TPU v7x, 256 devices: a whole 4x4x8 slice. The times are simulated.
256 devices in a mesh: row: 8 (over z_lo, x), col: 32 (over z_hi, y, core).
Axes of the slice: x: 4, y: 4, z: 8 (z_hi: 4, z_lo: 2; z = z_hi * 2 + z_lo), core: 2. Of those that a mesh axis runs over, the one named last changes fastest.
Arguments:
- wave_field: float32 [64, 128, 64, 128], P(None, 'col', 'row'), may hold values from -6 to 6
- medium_term: float32 [128, 64, 128], P('col', 'row'), may hold values from 0.5 to 4
- node_flux: float32 [64, 32, 8, 384], P(None, 'col', 'row'), may hold values from -6 to 6
- node_cell: int32 [32, 8, 384], P('col', 'row'), may hold values from 0 to 4095
- block_target: int32 [32, 8, 32], P('col', 'row'), may hold values from 0 to 31, as said below
- boundary_matrix: bfloat16 [2, 4096, 98304], P(None, 'row', 'col'), may hold values from -0.0390625 to 0.0390625
Outputs:
- volume_image: float32 [64, 128, 64, 128], P(None, 'col', 'row')
- boundary_image: float32 [4096, 64], P(('row', 'col'))
Inputs may be any that keep to these rules, and one draw needn't show every extreme that they name: For every brick (c, r), block_target[c, r, :] is a permutation of the 32 column blocks.
All inputs are finite; a program needn't handle non-finite values.
Results may differ from a plain program's by a relative error of at most 0.0029.
Values may be sent and summed in bfloat16 or wider, within the bound.
A program may use at most 64 MiB of HBM per device.

v0:
```python
import jax
import jax.numpy as jnp
from jax import lax
from jax.sharding import PartitionSpec as P


def in_order(tiles, dim):
    tiles = jnp.moveaxis(tiles, 0, dim)
    lengths = tiles.shape
    return tiles.reshape(*lengths[:dim], lengths[dim] * lengths[dim + 1], *lengths[dim + 2 :])


def sent_to_all(x, axis):
    count = lax.axis_size(axis)
    return lax.all_to_all(jnp.broadcast_to(x[None], (count, *x.shape)), axis, 0, 0, tiled=True)


def gather_directly(x, axis, dim):
    return in_order(sent_to_all(x, axis), dim)


def padded_2(block, sides, width):
    for axis, dim in sides:
        count = lax.axis_size(axis)
        forward = [(i, i + 1) for i in range(count - 1)]
        backward = [(target, source) for source, target in forward]
        low = lax.ppermute(
            lax.slice_in_dim(block, block.shape[dim] - width, None, axis=dim), axis, forward
        )
        high = lax.ppermute(lax.slice_in_dim(block, 0, width, axis=dim), axis, backward)
        block = jnp.concatenate([low, block, high], axis=dim)
    return block


def in_blocks(x, dim, count):
    lengths = x.shape
    tiles = x.reshape(*lengths[:dim], count, lengths[dim] // count, *lengths[dim + 1 :])
    return jnp.moveaxis(tiles, dim, 0)


def sum_at_owner(x, axis, dim):
    count = lax.axis_size(axis)
    tiles = lax.all_to_all(in_blocks(x, dim, count), axis, 0, 0, tiled=True)
    return jnp.sum(tiles, axis=0)


def three_tap(values, axis, side_weight, centre_weight):
    length = values.shape[axis]
    lower = lax.slice_in_dim(values, 0, length - 2, axis=axis)
    middle = lax.slice_in_dim(values, 1, length - 1, axis=axis)
    upper = lax.slice_in_dim(values, 2, length, axis=axis)
    return side_weight * (lower + upper) + centre_weight * middle


def on_device(wave_field, medium_term, node_flux, node_cell, block_target, boundary_matrix):
    components, width_x, width_y, depth_cells = wave_field.shape
    cell_total = width_x * width_y * depth_cells
    angles = components // 2
    col_count = lax.axis_size("col")
    node_total = node_cell.shape[-1]
    slot_len = node_total // col_count
    targets = block_target.reshape(col_count)
    block_ids = jnp.arange(col_count, dtype=jnp.int32)
    matches = targets[None, :] == block_ids[:, None]
    slot_cells = node_cell.reshape(col_count, slot_len)
    ordered = jnp.sum(jnp.where(matches[:, :, None], slot_cells[None, :, :], 0), axis=1).reshape(
        node_total
    )
    flat_field = wave_field.reshape(components, cell_total)
    traces = jnp.take(flat_field, ordered, axis=1).astype(jnp.bfloat16)
    received = lax.all_to_all(traces, "col", split_axis=1, concat_axis=1, tiled=True)
    column_traces = gather_directly(received, "row", 1)
    padded = padded_2(wave_field, (("row", 2), ("col", 1)), 1)
    padded = jnp.pad(padded, ((0, 0), (0, 0), (0, 0), (1, 1)))
    elem_z = three_tap(padded, 3, 1.0 / 6.0, 2.0 / 3.0)
    lapl_z = three_tap(padded, 3, -1.0, 2.0)
    lump_z = three_tap(padded, 3, 1.0 / 3.0, 2.0 / 3.0)
    elem_yz = three_tap(elem_z, 2, 1.0 / 6.0, 2.0 / 3.0)
    lapl_y_elem_z = three_tap(elem_z, 2, -1.0, 2.0)
    elem_y_lapl_z = three_tap(lapl_z, 2, 1.0 / 6.0, 2.0 / 3.0)
    lump_yz = three_tap(lump_z, 2, 1.0 / 3.0, 2.0 / 3.0)
    stiffness = three_tap(elem_yz, 1, -1.0, 2.0) + three_tap(
        lapl_y_elem_z + elem_y_lapl_z, 1, 1.0 / 6.0, 2.0 / 3.0
    )
    mass_sum = three_tap(lump_yz, 1, 1.0 / 3.0, 2.0 / 3.0)
    volume_image = stiffness - medium_term[None] * mass_sum
    flat_image = volume_image.reshape(components, cell_total)
    flat_image = flat_image.at[:, node_cell.reshape(node_total)].add(
        -node_flux.reshape(components, node_total)
    )
    volume_image = flat_image.reshape(components, width_x, width_y, depth_cells)
    slab_rows = boundary_matrix.shape[1]
    column_span = boundary_matrix.shape[2]
    own_rows = slab_rows // col_count
    products = lax.dot_general(
        boundary_matrix.reshape(2 * (own_rows * lax.axis_size("col")), column_span),
        column_traces,
        (((1,), (1,)), ((), ())),
        preferred_element_type=jnp.float32,
    )
    real_part = products[: own_rows * lax.axis_size("col")]
    imag_part = products[own_rows * lax.axis_size("col") :]
    boundary_image = sum_at_owner(
        jnp.concatenate(
            [
                real_part[:, :angles] - imag_part[:, angles:],
                imag_part[:, :angles] + real_part[:, angles:],
            ],
            axis=1,
        ),
        "col",
        0,
    )
    return (volume_image, boundary_image)


def solution(mesh):
    in_specs = (
        P(None, "col", "row", None),
        P("col", "row", None),
        P(None, "col", "row", None),
        P("col", "row", None),
        P("col", "row", None),
        P(None, "row", "col"),
    )
    out_specs = (P(None, "col", "row", None), P(("row", "col"), None))
    return jax.shard_map(
        on_device, mesh=mesh, in_specs=in_specs, out_specs=out_specs, check_vma=False
    )
```

profile of v0, /device:TPU:1, one launch (start us, length us, event | category | flops | bytes accessed | tf_op | source)
XLA Modules:
  0.0 84.1 jit_solution(6091311905287193799)
XLA Ops:
  0.7 2.1 %fusion.19 = (f32[64,4,1,128]{3,2,1,0:T(1,128)S(1)}, f32[64,4,1,128]{3,2,1,0:T(1,128)S(1)}) fusion(f32[64,4,8,128]{3,2,1,0:T(8,128)} %param.6), kind=kLoop, calls=%fused_computation.54 | loop fusion | bytes 524288 | tf_op jit(solution)/shard_map/slice | solution.py:28
  2.8 1.3 %collective-permute-start.1 = (f32[64,4,1,128]{3,0,2,1:T(8,128)S(1)}, f32[64,4,1,128]{3,0,2,1:T(8,128)S(1)}, u32[]{:S(2)}, u32[]{:S(2)}) collective-permute-start(f32[64,4,1,128]{3,0,2,1:T(8,128)S(1)} %copy.46), channel_id=1, source_target_pairs={{32,0},{64,32},{96,64},{128,96},{160,128},{192,160},{224,192},{33,... | collective-permute-start | bytes 393224 | tf_op jit(solution)/shard_map/ppermute | solution.py:30
  4.1 4.7 %collective-permute-start = (f32[64,4,1,128]{3,0,2,1:T(8,128)S(1)}, f32[64,4,1,128]{3,0,2,1:T(8,128)S(1)}, u32[]{:S(2)}, u32[]{:S(2)}) collective-permute-start(f32[64,4,1,128]{3,0,2,1:T(8,128)S(1)} %copy.45), channel_id=1, source_target_pairs={{0,32},{32,64},{64,96},{96,128},{128,160},{160,192},{192,224},{1,3... | collective-permute-start | bytes 393224 | tf_op jit(solution)/shard_map/ppermute | solution.py:27
  8.9 1.8 %copy.38 = bf16[64,4,8,128]{0,3,2,1:T(8,128)(2,1)S(1)} copy(f32[64,4,8,128]{3,2,1,0:T(8,128)} %param.6) | data formatting | bytes 1572864 | tf_op args[0]
  11.4 1.4 %gather_fusion = bf16[384,64]{1,0:T(8,128)(2,1)S(1)} fusion(bf16[64,4096]{0,1:T(8,128)(2,1)S(1)} %bitcast.32, s32[1024]{0:T(1024)S(1)} %pad_clamp_fusion), kind=kCustom, calls=%fused_computation | custom fusion | bytes 99840 | tf_op jit(solution)/shard_map/jit(_take)/gather | solution.py:70
  13.5 5.1 %collective-permute-start.3 = (f32[64,1,10,128]{3,2,1,0:T(8,128)S(1)}, f32[64,1,10,128]{3,2,1,0:T(8,128)S(1)}, u32[]{:S(2)}, u32[]{:S(2)}) collective-permute-start(f32[64,1,10,128]{3,2,1,0:T(8,128)S(1)} %get-tuple-element.16), channel_id=1, source_target_pairs={{1,0},{2,1},{3,2},{4,3},{5,4},{6,5},{7,6},{8,7},{9,8},{10,9},{11,1... | collective-permute-start | bytes 983048 | tf_op jit(solution)/shard_map/ppermute | solution.py:30
  18.6 1.9 %collective-permute-start.2 = (f32[64,1,10,128]{3,2,1,0:T(8,128)S(1)}, f32[64,1,10,128]{3,2,1,0:T(8,128)}, u32[]{:S(2)}, u32[]{:S(2)}) collective-permute-start(f32[64,1,10,128]{3,2,1,0:T(8,128)S(1)} %get-tuple-element.15), channel_id=1, source_target_pairs={{0,1},{1,2},{2,3},{3,4},{4,5},{5,6},{6,7},{7,8},{8,9},{9,10},{10,1... | collective-permute-start | bytes 983048 | tf_op jit(solution)/shard_map/ppermute | solution.py:27
  21.5 13.0 %all-to-all-start = ((bf16[32,2,384]{2,1,0:T(2,128)(2,1)}), bf16[32,2,384]{2,1,0:T(2,128)(2,1)S(1)}, u32[]{:S(2)}, u32[]{:S(2)}) async-start(bf16[32,2,384]{2,1,0:T(2,128)(2,1)} %reshape.153), calls=%async_computation | async-start | bytes 98304 | tf_op jit(solution)/shard_map/all_to_all | solution.py:71
  34.6 0.8 copy.47
  36.0 8.6 %all-to-all-done = bf16[32,2,384]{2,1,0:T(2,128)(2,1)S(1)} async-done(((bf16[32,2,384]{2,1,0:T(2,128)(2,1)}), bf16[32,2,384]{2,1,0:T(2,128)(2,1)S(1)}, u32[]{:S(2)}, u32[]{:S(2)}) %all-to-all-start) | async-done | bytes 49184 | tf_op jit(solution)/shard_map/all_to_all | solution.py:71
  44.9 0.8 broadcast_in_dim.51
  45.7 5.5 %all-to-all-start.1 = ((bf16[8,64,384]{2,1,0:T(8,128)(2,1)}), bf16[8,64,384]{2,1,0:T(8,128)(2,1)S(1)}, u32[]{:S(2)}, u32[]{:S(2)}) async-start(bf16[8,64,384]{2,1,0:T(8,128)(2,1)} %broadcast_in_dim.51), calls=%async_computation.1 | async-start | bytes 786432 | tf_op jit(solution)/shard_map/all_to_all | solution.py:15
  51.2 1.5 %pad_maximum_fusion = f32[64,6,10,128]{3,2,1,0:T(8,128)S(1)} fusion(f32[64,1,10,128]{3,2,1,0:T(8,128)S(1)} %collective-permute-done.3, f32[64,4,1,128]{3,2,1,0:T(1,128)S(1)} %copy.33, f32[64,4,8,128]{3,2,1,0:T(8,128)S(1)} %copy-done, f32[64,4,1,128]{3,2,1,0:T(1,128)S(1)} %copy.32, f32[64,1,10,128]{3,2,1,0:T(8,128)} %collective-permute-done.2), kind=kLoop, calls=%fused_computation.5 | loop fusion | flops 1966080 | bytes 3932160 | tf_op jit(solution)/shard_map/concatenate | solution.py:31
  52.7 5.0 %multiply_add_fusion.2 = (f32[64,6,10,128]{3,2,1,0:T(8,128)S(1)}, f32[64,6,10,128]{3,2,1,0:T(8,128)S(1)}, f32[64,6,10,128]{3,2,1,0:T(8,128)S(1)}) fusion(f32[64,6,10,128]{3,2,1,0:T(8,128)S(1)} %pad_maximum_fusion), kind=kLoop, calls=%fused_computation.8 | loop fusion | flops 5406720 | bytes 7864320 | tf_op jit(solution)/shard_map/add | solution.py:52
  57.7 1.6 %fusion.1 = f32[64,6,8,128]{3,2,1,0:T(8,128)} fusion(f32[64,6,10,128]{3,2,1,0:T(8,128)S(1)} %get-tuple-element.14), kind=kLoop, calls=%fused_computation.10 | loop fusion | flops 1572864 | bytes 6291456 | tf_op jit(solution)/shard_map/add | solution.py:52
  59.3 1.0 %multiply_add_fusion.3 = (f32[64,6,8,128]{3,2,1,0:T(8,128)S(1)}, f32[64,6,8,128]{3,2,1,0:T(8,128)S(1)}) fusion(f32[64,6,10,128]{3,2,1,0:T(8,128)S(1)} %get-tuple-element.12, f32[64,6,10,128]{3,2,1,0:T(8,128)S(1)} %get-tuple-element.13), kind=kLoop, calls=%fused_computation.19 | loop fusion | flops 4718592 | bytes 12582912 | tf_op jit(solution)/shard_map/add | solution.py:52
  60.4 4.8 %convolution_bitcast_fusion = f32[1024,64]{0,1:T(8,128)S(1)} fusion(bf16[64,3072]{1,0:T(8,128)(2,1)S(1)} %bitcast.34, bf16[1024,3072]{1,0:T(8,128)(2,1)} %bitcast.31), kind=kOutput, calls=%fused_computation.20 | convolution fusion | flops 402653184 | bytes 6946816 | tf_op jit(solution)/shard_map/dot_general | solution.py:95
  65.4 0.8 reshape.155
  66.2 4.2 %all-to-all-start.2 = ((f32[32,1,1024]{2,1,0:T(1,128)}), f32[32,1,1024]{2,1,0:T(1,128)S(1)}, u32[]{:S(2)}, u32[]{:S(2)}) async-start(f32[32,1,1024]{2,1,0:T(1,128)} %reshape.155), calls=%async_computation.2 | async-start | bytes 262144 | tf_op jit(solution)/shard_map/all_to_all | solution.py:43
  70.4 3.5 %fusion.8 = f32[64,4,8,128]{3,2,1,0:T(8,128)} fusion(f32[64,6,8,128]{3,2,1,0:T(8,128)} %fusion.1, f32[64,6,8,128]{3,2,1,0:T(8,128)S(1)} %get-tuple-element.11, f32[64,6,8,128]{3,2,1,0:T(8,128)S(1)} %get-tuple-element.10, f32[4,8,128]{2,1,0:T(8,128)S(1)} %copy-done.3), kind=kLoop, calls=%fused_computation.24 | loop fusion | flops 3932160 | bytes 10502144 | tf_op jit(solution)/shard_map/sub | solution.py:86
  73.9 1.9 %copy.34 = f32[64,4,8,128]{0,3,2,1:T(8,128)S(1)} copy(f32[64,4,8,128]{3,2,1,0:T(8,128)} %fusion.8) | data formatting | bytes 2097152 | tf_op jit(solution)/shard_map/sub | solution.py:86
  75.8 3.7 %scatter_custom_fusion = f32[64,4096]{0,1:T(8,128)S(1)} fusion(f32[64,4096]{0,1:T(8,128)S(1)} %bitcast.29, s32[384]{0:T(512)} %fusion.17, f32[64,1,1,384]{0,3,1,2:T(8,128)S(1)} %copy-done.1), kind=kCustom, calls=%fused_computation.40 | custom fusion | flops 24576 | bytes 1245184 | tf_op jit(solution)/shard_map/scatter-add | solution.py:88
  79.5 1.8 %copy.43 = f32[64,4,8,128]{3,2,1,0:T(8,128)} copy(f32[64,4,8,128]{0,3,2,1:T(8,128)S(1)} %bitcast.30) | data formatting | bytes 2097152
  82.4 0.9 %reduce.5 = f32[32,1024]{1,0:T(8,128)S(1)} reduce(f32[32,1,1024]{2,1,0:T(1,128)S(1)} %all-to-all-done.2, f32[]{:T(128)} %broadcast.88), dimensions={1}, to_apply=%all_to_all.12.reduce_sub_computation | reduce | bytes 262148 | tf_op jit(solution)/shard_map/all_to_all | solution.py:43
  (49 shorter events, 5.3 us)
Async XLA Ops:
  0.6 12.7 %copy-start = (f32[64,4,8,128]{3,2,1,0:T(8,128)S(1)}, f32[64,4,8,128]{3,2,1,0:T(8,128)}, u32[]{:S(2)}) copy-start(f32[64,4,8,128]{3,2,1,0:T(8,128)} %param.6) | copy-start | bytes 3145732
  0.6 10.0 %copy-start.4 = (s32[1,1,384]{2,1,0:T(1,128)S(1)}, s32[1,1,384]{2,1,0:T(1,128)}, u32[]{:S(2)}) copy-start(s32[1,1,384]{2,1,0:T(1,128)} %param.9) | copy-start | bytes 4612
  0.7 10.2 %copy-start.5 = (s32[1,1,32]{2,1,0:T(1,128)S(1)}, s32[1,1,32]{2,1,0:T(1,128)}, u32[]{:S(2)}) copy-start(s32[1,1,32]{2,1,0:T(1,128)} %param.10) | copy-start | bytes 388
  2.8 10.2 %collective-permute-start.1 = (f32[64,4,1,128]{3,0,2,1:T(8,128)S(1)}, f32[64,4,1,128]{3,0,2,1:T(8,128)S(1)}, u32[]{:S(2)}, u32[]{:S(2)}) collective-permute-start(f32[64,4,1,128]{3,0,2,1:T(8,128)S(1)} %copy.46), channel_id=1, source_target_pairs={{32,0},{64,32},{96,64},{128,96},{160,128},{192,160},{224,192},{33,... | collective-permute-start | bytes 393224 | tf_op jit(solution)/shard_map/ppermute | solution.py:30
  4.1 30.3 %copy-start.2 = (f32[64,1,1,384]{3,2,1,0:T(1,128)S(1)}, f32[64,1,1,384]{3,2,1,0:T(1,128)}, u32[]{:S(2)}) copy-start(f32[64,1,1,384]{3,2,1,0:T(1,128)} %param.8) | copy-start | bytes 294916
  4.1 9.0 %collective-permute-start = (f32[64,4,1,128]{3,0,2,1:T(8,128)S(1)}, f32[64,4,1,128]{3,0,2,1:T(8,128)S(1)}, u32[]{:S(2)}, u32[]{:S(2)}) collective-permute-start(f32[64,4,1,128]{3,0,2,1:T(8,128)S(1)} %copy.45), channel_id=1, source_target_pairs={{0,32},{32,64},{64,96},{96,128},{128,160},{160,192},{192,224},{1,3... | collective-permute-start | bytes 393224 | tf_op jit(solution)/shard_map/ppermute | solution.py:27
  13.5 37.6 %collective-permute-start.3 = (f32[64,1,10,128]{3,2,1,0:T(8,128)S(1)}, f32[64,1,10,128]{3,2,1,0:T(8,128)S(1)}, u32[]{:S(2)}, u32[]{:S(2)}) collective-permute-start(f32[64,1,10,128]{3,2,1,0:T(8,128)S(1)} %get-tuple-element.16), channel_id=1, source_target_pairs={{1,0},{2,1},{3,2},{4,3},{5,4},{6,5},{7,6},{8,7},{9,8},{10,9},{11,1... | collective-permute-start | bytes 983048 | tf_op jit(solution)/shard_map/ppermute | solution.py:30
  18.6 32.5 %collective-permute-start.2 = (f32[64,1,10,128]{3,2,1,0:T(8,128)S(1)}, f32[64,1,10,128]{3,2,1,0:T(8,128)}, u32[]{:S(2)}, u32[]{:S(2)}) collective-permute-start(f32[64,1,10,128]{3,2,1,0:T(8,128)S(1)} %get-tuple-element.15), channel_id=1, source_target_pairs={{0,1},{1,2},{2,3},{3,4},{4,5},{5,6},{6,7},{7,8},{8,9},{9,10},{10,1... | collective-permute-start | bytes 983048 | tf_op jit(solution)/shard_map/ppermute | solution.py:27
  21.5 23.2 %all-to-all-start = ((bf16[32,2,384]{2,1,0:T(2,128)(2,1)}), bf16[32,2,384]{2,1,0:T(2,128)(2,1)S(1)}, u32[]{:S(2)}, u32[]{:S(2)}) async-start(bf16[32,2,384]{2,1,0:T(2,128)(2,1)} %reshape.153), calls=%async_computation | async-start | bytes 98304 | tf_op jit(solution)/shard_map/all_to_all | solution.py:71
  45.7 14.6 %all-to-all-start.1 = ((bf16[8,64,384]{2,1,0:T(8,128)(2,1)}), bf16[8,64,384]{2,1,0:T(8,128)(2,1)S(1)}, u32[]{:S(2)}, u32[]{:S(2)}) async-start(bf16[8,64,384]{2,1,0:T(8,128)(2,1)} %broadcast_in_dim.51), calls=%async_computation.1 | async-start | bytes 786432 | tf_op jit(solution)/shard_map/all_to_all | solution.py:15
  60.4 10.0 %copy-start.3 = (f32[4,8,128]{2,1,0:T(8,128)S(1)}, f32[4,8,128]{2,1,0:T(8,128)}, u32[]{:S(2)}) copy-start(f32[4,8,128]{2,1,0:T(8,128)} %param.7) | copy-start | bytes 49156
  66.2 15.7 %all-to-all-start.2 = ((f32[32,1,1024]{2,1,0:T(1,128)}), f32[32,1,1024]{2,1,0:T(1,128)S(1)}, u32[]{:S(2)}, u32[]{:S(2)}) async-start(f32[32,1,1024]{2,1,0:T(1,128)} %reshape.155), calls=%async_computation.2 | async-start | bytes 262144 | tf_op jit(solution)/shard_map/all_to_all | solution.py:43
  73.9 1.9 %copy-start.1 = (f32[64,1,1,384]{0,3,1,2:T(8,128)S(1)}, f32[64,1,1,384]{0,3,1,2:T(8,128)}, u32[]{:S(2)}) copy-start(f32[64,1,1,384]{0,3,1,2:T(8,128)} %copy.47) | copy-start | bytes 294916
where the time goes:
time: 84.7 us; the launch traced here: 84.1 us
  starting transfers between devices  35.6 us (42%)
  other arithmetic  19.3 us (23%)
  local copies, waits for them, and re-layouts  14.1 us (17%)
  waiting for transfers between devices  9.24 us (11%)
  matrix products  4.81 us (6%)
  between operations  0.99 us (1%)
    all_to_all x1, starting transfers between devices, on_device(): lax.all_to_all(traces, 'col', split_axis=1, concat_axis=1, tiled=True)  13 us
    all_to_all x1, waiting for transfers between devices, on_device(): lax.all_to_all(traces, 'col', split_axis=1, concat_axis=1, tiled=True)  8.63 us
    add x3, other arithmetic, three_tap(): return side_weight * (lower + upper) + centre_weight * middle  7.61 us
    ppermute x2, starting transfers between devices, padded_2(): lax.ppermute(lax.slice_in_dim(block, block.shape[dim] - width, None, axis...  6.62 us
    ppermute x2, starting transfers between devices, padded_2(): lax.ppermute(lax.slice_in_dim(block, 0, width, axis=dim), axis, backward)  6.39 us
    all_to_all x1, starting transfers between devices, sent_to_all(): lax.all_to_all(jnp.broadcast_to(x[None], (count, *x.shape)), axis, 0, 0,...  5.45 us
    unnamed x20, local copies, waits for them, and re-layouts  5.44 us
    dot_general x1, matrix products, on_device(): lax.dot_general(boundary_matrix.reshape(2 * (own_rows * lax.axis_size('co...  4.81 us
  transfers between devices with their start and end apart: 7, of which 2 were waited for; matrix products, arithmetic and copies ran while one was open for 33% of the time, Pallas kernels for 0%

commit v1 on v0

--- a/solution.py
+++ b/solution.py
@@ -68,7 +68,10 @@
     )
     flat_field = wave_field.reshape(components, cell_total)
     traces = jnp.take(flat_field, ordered, axis=1).astype(jnp.bfloat16)
-    received = lax.all_to_all(traces, "col", split_axis=1, concat_axis=1, tiled=True)
+    peers = lax.axis_size("col")
+    shards = jnp.stack(jnp.split(traces, peers, axis=1), axis=0)
+    shards = lax.all_to_all(shards, "col", split_axis=0, concat_axis=0)
+    received = jnp.concatenate(shards, axis=1)
     column_traces = gather_directly(received, "row", 1)
     padded = padded_2(wave_field, (("row", 2), ("col", 1)), 1)
     padded = jnp.pad(padded, ((0, 0), (0, 0), (0, 0), (1, 1)))

time: 84.7 us -> 91.3 us (1.078)
  starting transfers between devices: 35.6 us -> 48.9 us
  waiting for transfers between devices: 9.24 us -> 2.16 us
    all_to_all x1, starting transfers between devices: 4.16 us -> 18.9 us  [sum_at_owner(): tiles = lax.all_to_all(in_blocks(x, dim, count), axis, 0, 0, tiled=True)]
    all_to_all x1, waiting for transfers between devices: 8.63 us -> 2.14 us  [on_device(): shards = lax.all_to_all(shards, 'col', split_axis=0, concat_axis=0)]
    ppermute x2, starting transfers between devices: 6.39 us -> 3.44 us  [padded_2(): lax.ppermute(lax.slice_in_dim(block, 0, width, axis=dim), axis, backward)]
    ppermute x2, starting transfers between devices: 6.62 us -> 7.99 us  [padded_2(): lax.ppermute(lax.slice_in_dim(block, block.shape[dim] - width, None, axis...]
    unnamed x20 -> x51, local copies, waits for them, and re-layouts: 5.44 us -> 5.76 us
  transfers between devices with their start and end apart: 7 -> 7, of which waited for: 2 -> 1; matrix products, arithmetic and copies ran while one was open for 33% -> 31% of each run, Pallas kernels for 0% -> 0%
where the time goes in v1:
time: 91.3 us; the launch traced here: 90.7 us
  starting transfers between devices  48.9 us (54%)
  other arithmetic  19.3 us (21%)
  local copies, waits for them, and re-layouts  14.5 us (16%)
  matrix products  4.81 us (5%)
  waiting for transfers between devices  2.16 us (2%)
  between operations  1.07 us (1%)
    all_to_all x1, starting transfers between devices, sum_at_owner(): tiles = lax.all_to_all(in_blocks(x, dim, count), axis, 0, 0, tiled=True)  18.9 us
    all_to_all x1, starting transfers between devices, on_device(): shards = lax.all_to_all(shards, 'col', split_axis=0, concat_axis=0)  12.7 us
    ppermute x2, starting transfers between devices, padded_2(): lax.ppermute(lax.slice_in_dim(block, block.shape[dim] - width, None, axis...  7.99 us
    add x3, other arithmetic, three_tap(): return side_weight * (lower + upper) + centre_weight * middle  7.61 us
    all_to_all x1, starting transfers between devices, sent_to_all(): lax.all_to_all(jnp.broadcast_to(x[None], (count, *x.shape)), axis, 0, 0,...  5.86 us
    unnamed x51, local copies, waits for them, and re-layouts  5.76 us
    dot_general x1, matrix products, on_device(): lax.dot_general(boundary_matrix.reshape(2 * (own_rows * lax.axis_size('co...  4.81 us
    scatter-add x1, other arithmetic, on_device(): flat_image.at[:, node_cell.reshape(node_total)]  3.7 us
  transfers between devices with their start and end apart: 7, of which 1 were waited for; matrix products, arithmetic and copies ran while one was open for 31% of the time, Pallas kernels for 0%

profile of v1, /device:TPU:1, one launch (start us, length us, event | category | flops | bytes accessed | tf_op | source)
XLA Modules:
  0.0 90.7 jit_solution(7664783763376845179)
XLA Ops:
  0.7 2.1 %fusion.20 = (f32[64,4,1,128]{3,2,1,0:T(1,128)S(1)}, f32[64,4,1,128]{3,2,1,0:T(1,128)S(1)}) fusion(f32[64,4,8,128]{3,2,1,0:T(8,128)} %param.6), kind=kLoop, calls=%fused_computation.119 | loop fusion | bytes 524288 | tf_op jit(solution)/shard_map/slice | solution.py:28
  2.8 1.3 %collective-permute-start.1 = (f32[64,4,1,128]{3,0,2,1:T(8,128)S(1)}, f32[64,4,1,128]{3,0,2,1:T(8,128)S(1)}, u32[]{:S(2)}, u32[]{:S(2)}) collective-permute-start(f32[64,4,1,128]{3,0,2,1:T(8,128)S(1)} %copy.46), channel_id=1, source_target_pairs={{32,0},{64,32},{96,64},{128,96},{160,128},{192,160},{224,192},{33,... | collective-permute-start | bytes 393224 | tf_op jit(solution)/shard_map/ppermute | solution.py:30
  4.1 4.6 %collective-permute-start = (f32[64,4,1,128]{3,0,2,1:T(8,128)S(1)}, f32[64,4,1,128]{3,0,2,1:T(8,128)S(1)}, u32[]{:S(2)}, u32[]{:S(2)}) collective-permute-start(f32[64,4,1,128]{3,0,2,1:T(8,128)S(1)} %copy.45), channel_id=1, source_target_pairs={{0,32},{32,64},{64,96},{96,128},{128,160},{160,192},{192,224},{1,3... | collective-permute-start | bytes 393224 | tf_op jit(solution)/shard_map/ppermute | solution.py:27
  8.7 1.8 %copy.38 = bf16[64,4,8,128]{0,3,2,1:T(8,128)(2,1)S(1)} copy(f32[64,4,8,128]{3,2,1,0:T(8,128)} %param.6) | data formatting | bytes 1572864 | tf_op args[0]
  11.4 1.4 %gather_fusion = bf16[384,64]{1,0:T(8,128)(2,1)S(1)} fusion(bf16[64,4096]{0,1:T(8,128)(2,1)S(1)} %bitcast.161, s32[1024]{0:T(1024)S(1)} %pad_clamp_fusion), kind=kCustom, calls=%fused_computation | custom fusion | bytes 99840 | tf_op jit(solution)/shard_map/jit(_take)/gather | solution.py:70
  14.2 12.7 %all-to-all-start = ((bf16[32,2,384]{2,1,0:T(2,128)(2,1)}), bf16[32,2,384]{2,1,0:T(2,128)(2,1)S(1)}, u32[]{:S(2)}, u32[]{:S(2)}) async-start(bf16[32,2,384]{2,1,0:T(2,128)(2,1)} %reshape.152), calls=%async_computation | async-start | bytes 98304 | tf_op jit(solution)/shard_map/all_to_all | solution.py:73
  27.0 0.8 copy.47
  28.3 2.1 %collective-permute-start.3 = (f32[64,1,10,128]{3,2,1,0:T(8,128)S(1)}, f32[64,1,10,128]{3,2,1,0:T(8,128)S(1)}, u32[]{:S(2)}, u32[]{:S(2)}) collective-permute-start(f32[64,1,10,128]{3,2,1,0:T(8,128)S(1)} %get-tuple-element.16), channel_id=1, source_target_pairs={{1,0},{2,1},{3,2},{4,3},{5,4},{6,5},{7,6},{8,7},{9,8},{10,9},{11,1... | collective-permute-start | bytes 983048 | tf_op jit(solution)/shard_map/ppermute | solution.py:30
  30.5 3.4 %collective-permute-start.2 = (f32[64,1,10,128]{3,2,1,0:T(8,128)S(1)}, f32[64,1,10,128]{3,2,1,0:T(8,128)}, u32[]{:S(2)}, u32[]{:S(2)}) collective-permute-start(f32[64,1,10,128]{3,2,1,0:T(8,128)S(1)} %get-tuple-element.15), channel_id=1, source_target_pairs={{0,1},{1,2},{2,3},{3,4},{4,5},{5,6},{6,7},{7,8},{8,9},{9,10},{10,1... | collective-permute-start | bytes 983048 | tf_op jit(solution)/shard_map/ppermute | solution.py:27
  34.5 2.1 %all-to-all-done = bf16[32,2,384]{2,1,0:T(2,128)(2,1)S(1)} async-done(((bf16[32,2,384]{2,1,0:T(2,128)(2,1)}), bf16[32,2,384]{2,1,0:T(2,128)(2,1)S(1)}, u32[]{:S(2)}, u32[]{:S(2)}) %all-to-all-start) | async-done | bytes 49184 | tf_op jit(solution)/shard_map/all_to_all | solution.py:73
  37.0 0.8 broadcast_in_dim.50
  37.8 5.9 %all-to-all-start.1 = ((bf16[8,64,384]{2,1,0:T(8,128)(2,1)}), bf16[8,64,384]{2,1,0:T(8,128)(2,1)S(1)}, u32[]{:S(2)}, u32[]{:S(2)}) async-start(bf16[8,64,384]{2,1,0:T(8,128)(2,1)} %broadcast_in_dim.50), calls=%async_computation.1 | async-start | bytes 786432 | tf_op jit(solution)/shard_map/all_to_all | solution.py:15
  43.6 1.5 %pad_maximum_fusion = f32[64,6,10,128]{3,2,1,0:T(8,128)S(1)} fusion(f32[64,1,10,128]{3,2,1,0:T(8,128)S(1)} %collective-permute-done.3, f32[64,4,1,128]{3,2,1,0:T(1,128)S(1)} %copy.33, f32[64,4,8,128]{3,2,1,0:T(8,128)S(1)} %copy-done, f32[64,4,1,128]{3,2,1,0:T(1,128)S(1)} %copy.32, f32[64,1,10,128]{3,2,1,0:T(8,128)} %collective-permute-done.2), kind=kLoop, calls=%fused_computation.5 | loop fusion | flops 1966080 | bytes 3932160 | tf_op jit(solution)/shard_map/concatenate | solution.py:31
  45.2 5.0 %multiply_add_fusion.2 = (f32[64,6,10,128]{3,2,1,0:T(8,128)S(1)}, f32[64,6,10,128]{3,2,1,0:T(8,128)S(1)}, f32[64,6,10,128]{3,2,1,0:T(8,128)S(1)}) fusion(f32[64,6,10,128]{3,2,1,0:T(8,128)S(1)} %pad_maximum_fusion), kind=kLoop, calls=%fused_computation.8 | loop fusion | flops 5406720 | bytes 7864320 | tf_op jit(solution)/shard_map/add | solution.py:52
  50.2 1.6 %fusion.1 = f32[64,6,8,128]{3,2,1,0:T(8,128)} fusion(f32[64,6,10,128]{3,2,1,0:T(8,128)S(1)} %get-tuple-element.14), kind=kLoop, calls=%fused_computation.10 | loop fusion | flops 1572864 | bytes 6291456 | tf_op jit(solution)/shard_map/add | solution.py:52
  51.8 1.0 %multiply_add_fusion.3 = (f32[64,6,8,128]{3,2,1,0:T(8,128)S(1)}, f32[64,6,8,128]{3,2,1,0:T(8,128)S(1)}) fusion(f32[64,6,10,128]{3,2,1,0:T(8,128)S(1)} %get-tuple-element.12, f32[64,6,10,128]{3,2,1,0:T(8,128)S(1)} %get-tuple-element.13), kind=kLoop, calls=%fused_computation.19 | loop fusion | flops 4718592 | bytes 12582912 | tf_op jit(solution)/shard_map/add | solution.py:52
  52.8 4.8 %convolution_bitcast_fusion = f32[1024,64]{0,1:T(8,128)S(1)} fusion(bf16[64,3072]{1,0:T(8,128)(2,1)S(1)} %bitcast.163, bf16[1024,3072]{1,0:T(8,128)(2,1)} %bitcast.160), kind=kOutput, calls=%fused_computation.20 | convolution fusion | flops 402653184 | bytes 6946816 | tf_op jit(solution)/shard_map/dot_general | solution.py:98
  57.8 0.8 reshape.154
  58.7 18.9 %all-to-all-start.2 = ((f32[32,1,1024]{2,1,0:T(1,128)}), f32[32,1,1024]{2,1,0:T(1,128)S(1)}, u32[]{:S(2)}, u32[]{:S(2)}) async-start(f32[32,1,1024]{2,1,0:T(1,128)} %reshape.154), calls=%async_computation.2 | async-start | bytes 262144 | tf_op jit(solution)/shard_map/all_to_all | solution.py:43
  77.6 3.5 %fusion.8 = f32[64,4,8,128]{3,2,1,0:T(8,128)} fusion(f32[64,6,8,128]{3,2,1,0:T(8,128)} %fusion.1, f32[64,6,8,128]{3,2,1,0:T(8,128)S(1)} %get-tuple-element.11, f32[64,6,8,128]{3,2,1,0:T(8,128)S(1)} %get-tuple-element.10, f32[4,8,128]{2,1,0:T(8,128)S(1)} %copy-done.3), kind=kLoop, calls=%fused_computation.24 | loop fusion | flops 3932160 | bytes 10502144 | tf_op jit(solution)/shard_map/sub | solution.py:89
  81.1 1.9 %copy.34 = f32[64,4,8,128]{0,3,2,1:T(8,128)S(1)} copy(f32[64,4,8,128]{3,2,1,0:T(8,128)} %fusion.8) | data formatting | bytes 2097152 | tf_op jit(solution)/shard_map/sub | solution.py:89
  83.1 3.7 %scatter_custom_fusion = f32[64,4096]{0,1:T(8,128)S(1)} fusion(f32[64,4096]{0,1:T(8,128)S(1)} %bitcast.158, s32[384]{0:T(512)} %fusion.18, f32[64,1,1,384]{0,3,1,2:T(8,128)S(1)} %copy-done.1), kind=kCustom, calls=%fused_computation.39 | custom fusion | flops 24576 | bytes 1245184 | tf_op jit(solution)/shard_map/scatter-add | solution.py:91
  86.8 1.8 %copy.43 = f32[64,4,8,128]{3,2,1,0:T(8,128)} copy(f32[64,4,8,128]{0,3,2,1:T(8,128)S(1)} %bitcast.159) | data formatting | bytes 2097152
  89.0 0.9 %reduce.5 = f32[32,1024]{1,0:T(8,128)S(1)} reduce(f32[32,1,1024]{2,1,0:T(1,128)S(1)} %all-to-all-done.2, f32[]{:T(128)} %broadcast.86), dimensions={1}, to_apply=%all_to_all.11.reduce_sub_computation | reduce | bytes 262148 | tf_op jit(solution)/shard_map/all_to_all | solution.py:43
  (81 shorter events, 5.0 us)
Async XLA Ops:
  0.6 27.5 %copy-start = (f32[64,4,8,128]{3,2,1,0:T(8,128)S(1)}, f32[64,4,8,128]{3,2,1,0:T(8,128)}, u32[]{:S(2)}) copy-start(f32[64,4,8,128]{3,2,1,0:T(8,128)} %param.6) | copy-start | bytes 3145732
  0.6 9.9 %copy-start.4 = (s32[1,1,384]{2,1,0:T(1,128)S(1)}, s32[1,1,384]{2,1,0:T(1,128)}, u32[]{:S(2)}) copy-start(s32[1,1,384]{2,1,0:T(1,128)} %param.9) | copy-start | bytes 4612
  0.7 10.1 %copy-start.5 = (s32[1,1,32]{2,1,0:T(1,128)S(1)}, s32[1,1,32]{2,1,0:T(1,128)}, u32[]{:S(2)}) copy-start(s32[1,1,32]{2,1,0:T(1,128)} %param.10) | copy-start | bytes 388
  0.7 26.2 %copy-start.2 = (f32[64,1,1,384]{3,2,1,0:T(1,128)S(1)}, f32[64,1,1,384]{3,2,1,0:T(1,128)}, u32[]{:S(2)}) copy-start(f32[64,1,1,384]{3,2,1,0:T(1,128)} %param.8) | copy-start | bytes 294916
  2.8 25.0 %collective-permute-start.1 = (f32[64,4,1,128]{3,0,2,1:T(8,128)S(1)}, f32[64,4,1,128]{3,0,2,1:T(8,128)S(1)}, u32[]{:S(2)}, u32[]{:S(2)}) collective-permute-start(f32[64,4,1,128]{3,0,2,1:T(8,128)S(1)} %copy.46), channel_id=1, source_target_pairs={{32,0},{64,32},{96,64},{128,96},{160,128},{192,160},{224,192},{33,... | collective-permute-start | bytes 393224 | tf_op jit(solution)/shard_map/ppermute | solution.py:30
  4.1 23.8 %collective-permute-start = (f32[64,4,1,128]{3,0,2,1:T(8,128)S(1)}, f32[64,4,1,128]{3,0,2,1:T(8,128)S(1)}, u32[]{:S(2)}, u32[]{:S(2)}) collective-permute-start(f32[64,4,1,128]{3,0,2,1:T(8,128)S(1)} %copy.45), channel_id=1, source_target_pairs={{0,32},{32,64},{64,96},{96,128},{128,160},{160,192},{192,224},{1,3... | collective-permute-start | bytes 393224 | tf_op jit(solution)/shard_map/ppermute | solution.py:27
  14.2 22.5 %all-to-all-start = ((bf16[32,2,384]{2,1,0:T(2,128)(2,1)}), bf16[32,2,384]{2,1,0:T(2,128)(2,1)S(1)}, u32[]{:S(2)}, u32[]{:S(2)}) async-start(bf16[32,2,384]{2,1,0:T(2,128)(2,1)} %reshape.152), calls=%async_computation | async-start | bytes 98304 | tf_op jit(solution)/shard_map/all_to_all | solution.py:73
  28.3 15.3 %collective-permute-start.3 = (f32[64,1,10,128]{3,2,1,0:T(8,128)S(1)}, f32[64,1,10,128]{3,2,1,0:T(8,128)S(1)}, u32[]{:S(2)}, u32[]{:S(2)}) collective-permute-start(f32[64,1,10,128]{3,2,1,0:T(8,128)S(1)} %get-tuple-element.16), channel_id=1, source_target_pairs={{1,0},{2,1},{3,2},{4,3},{5,4},{6,5},{7,6},{8,7},{9,8},{10,9},{11,1... | collective-permute-start | bytes 983048 | tf_op jit(solution)/shard_map/ppermute | solution.py:30
  30.5 13.1 %collective-permute-start.2 = (f32[64,1,10,128]{3,2,1,0:T(8,128)S(1)}, f32[64,1,10,128]{3,2,1,0:T(8,128)}, u32[]{:S(2)}, u32[]{:S(2)}) collective-permute-start(f32[64,1,10,128]{3,2,1,0:T(8,128)S(1)} %get-tuple-element.15), channel_id=1, source_target_pairs={{0,1},{1,2},{2,3},{3,4},{4,5},{5,6},{6,7},{7,8},{8,9},{9,10},{10,1... | collective-permute-start | bytes 983048 | tf_op jit(solution)/shard_map/ppermute | solution.py:27
  37.8 15.0 %all-to-all-start.1 = ((bf16[8,64,384]{2,1,0:T(8,128)(2,1)}), bf16[8,64,384]{2,1,0:T(8,128)(2,1)S(1)}, u32[]{:S(2)}, u32[]{:S(2)}) async-start(bf16[8,64,384]{2,1,0:T(8,128)(2,1)} %broadcast_in_dim.50), calls=%async_computation.1 | async-start | bytes 786432 | tf_op jit(solution)/shard_map/all_to_all | solution.py:15
  52.8 24.8 %copy-start.3 = (f32[4,8,128]{2,1,0:T(8,128)S(1)}, f32[4,8,128]{2,1,0:T(8,128)}, u32[]{:S(2)}) copy-start(f32[4,8,128]{2,1,0:T(8,128)} %param.7) | copy-start | bytes 49156
  58.7 29.9 %all-to-all-start.2 = ((f32[32,1,1024]{2,1,0:T(1,128)}), f32[32,1,1024]{2,1,0:T(1,128)S(1)}, u32[]{:S(2)}, u32[]{:S(2)}) async-start(f32[32,1,1024]{2,1,0:T(1,128)} %reshape.154), calls=%async_computation.2 | async-start | bytes 262144 | tf_op jit(solution)/shard_map/all_to_all | solution.py:43
  81.1 1.9 %copy-start.1 = (f32[64,1,1,384]{0,3,1,2:T(8,128)S(1)}, f32[64,1,1,384]{0,3,1,2:T(8,128)}, u32[]{:S(2)}) copy-start(f32[64,1,1,384]{0,3,1,2:T(8,128)} %copy.47) | copy-start | bytes 294916
